TPU v7x, 256 devices: a whole 4x4x8 slice. The times are simulated.
256 devices in a mesh: seq: 64 (over z, x, core), tp: 4 (over y).
Axes of the slice: x: 4, y: 4, z: 8, core: 2. Of those that a mesh axis runs over, the one named last changes fastest.
Arguments:
- tokens: bfloat16 [32768, 2048], P('seq', 'tp'), may hold values from -6 to 6
- norm_gain: float32 [2048], replicated, may hold values from 0.1 to 1.9
- w_query: bfloat16 [2048, 2048], P(None, 'tp'), may hold values from -0.125 to 0.125
- w_keyval: bfloat16 [2048, 256], replicated, may hold values from -0.125 to 0.125
- w_out: bfloat16 [2048, 2048], P('tp'), may hold values from -0.5 to 0.5
- span_lens: int32 [64], P('seq'), may hold values from 1 to 512, 24576 in all
- cached_lens: int32 [64], P('seq'), may hold values from 1 to 1536, 49152 in all
- old_table: int32 [64, 64], P('seq'), may hold values from 0 to 63, each once within a row
- new_table: int32 [64, 64], P('seq'), may hold values from 0 to 63, each once within a row
- old_cache: bfloat16 [4096, 32, 256], P('seq', 'tp'), may hold values from -720 to 720
Outputs:
- mixed: bfloat16 [32768, 2048], P('seq', 'tp')
- new_cache: bfloat16 [4096, 32, 256], P('seq', 'tp')
Inputs may be any that keep to these rules, and one draw needn't show every extreme that they name: Request r's new tokens are the first span_lens[r] of its 512 rows. `old_table`: each row names every device once: each device holds exactly one block of every request. `new_table`: each row names every device once: each device receives exactly one block of every request.
All inputs are finite; a program needn't handle non-finite values. No bound on the sum of `span_lens` or of `cached_lens` on one device may be relied on, other than what follows from the above.
Results may differ from a plain program's by a relative error of at most 0.012.
The roundings to bfloat16 on the way count: a program that leaves them out, or rounds other values in their place, can miss the bound.
Values may be sent and summed in bfloat16 or wider, within the bound.
A program may use at most 128 MiB of HBM per device.

v0:
```python
import jax
import jax.numpy as jnp
from jax import lax
from jax.sharding import PartitionSpec as P

EPSILON = 1e-05
MASKED = -1e30


def normalize(rows, norm_gain):
    values = rows.astype(jnp.float32)
    average = jnp.mean(values, axis=1, keepdims=True)
    centred = values - average
    spread = jnp.mean(centred * centred, axis=1, keepdims=True)
    return (centred * lax.rsqrt(spread + EPSILON) * norm_gain).astype(jnp.bfloat16)


def body(
    tokens,
    norm_gain,
    w_query,
    w_keyval,
    w_out,
    span_lens,
    cached_lens,
    old_table,
    new_table,
    old_cache,
):
    full_rows = lax.all_gather(tokens, "tp", axis=1, tiled=True)
    normed = normalize(full_rows, norm_gain)
    query = jnp.dot(normed, w_query, preferred_element_type=jnp.float32).astype(jnp.bfloat16)
    keyval = jnp.dot(normed, w_keyval, preferred_element_type=jnp.float32).astype(jnp.bfloat16)
    groups = lax.axis_size("seq")
    tp_count = lax.axis_size("tp")
    holders = old_table[0]
    pooled = lax.all_gather(old_cache, "tp", axis=1, tiled=True)
    arrived = lax.all_to_all(pooled, "seq", split_axis=0, concat_axis=0, tiled=True)
    ordered = jnp.take(arrived, holders, axis=0)
    block_rows = ordered.shape[1]
    width = ordered.shape[2]
    capacity = groups * block_rows
    cached = ordered.reshape(capacity, width)
    held_len = cached_lens[0]
    span_len = span_lens[0]
    tok_rows = tokens.shape[0]
    share = block_rows // tp_count
    targets = new_table[0]
    device_ids = lax.broadcasted_iota(jnp.int32, (groups, groups), 0)
    block_ids = lax.broadcasted_iota(jnp.int32, (groups, groups), 1)
    matches = targets[None, :] == device_ids
    sources = jnp.sum(jnp.where(matches, block_ids, 0), axis=1)
    positions = lax.broadcasted_iota(jnp.int32, (capacity, 1), 0)
    placed = lax.dynamic_update_slice(cached, keyval, (held_len, jnp.int32(0)))
    fresh = jnp.where(positions < held_len + span_len, placed, jnp.zeros_like(placed))
    head_size = width // 2
    keys = fresh[:, :head_size]
    values = fresh[:, head_size:]
    local_heads = query.shape[1] // head_size
    query3 = query.reshape(tok_rows, local_heads, head_size)
    scores = jnp.einsum(
        "thd,kd->htk", query3, keys, preferred_element_type=jnp.float32
    ) * head_size ** (-0.5)
    row_pos = lax.broadcasted_iota(jnp.int32, (tok_rows, 1), 0)
    key_pos = lax.broadcasted_iota(jnp.int32, (1, capacity), 1)
    allowed = key_pos <= held_len + row_pos
    scores = jnp.where(allowed[None], scores, MASKED)
    top = jnp.max(scores, axis=2, keepdims=True)
    weights = jnp.exp(scores - top)
    probs = (weights / jnp.sum(weights, axis=2, keepdims=True)).astype(jnp.bfloat16)
    context = jnp.einsum("htk,kd->thd", probs, values, preferred_element_type=jnp.float32).astype(
        jnp.bfloat16
    )
    context = context.reshape(tok_rows, local_heads * head_size)
    partial_out = jnp.dot(context, w_out, preferred_element_type=jnp.float32)
    summed = lax.psum_scatter(
        partial_out.astype(jnp.bfloat16), "tp", scatter_dimension=1, tiled=True
    ).astype(jnp.float32)
    total = tokens.astype(jnp.float32) + summed
    mixed = jnp.where(row_pos < span_len, total, jnp.zeros_like(total)).astype(jnp.bfloat16)
    mine_part = lax.dynamic_slice_in_dim(
        fresh.reshape(groups, block_rows, width), lax.axis_index("tp") * share, share, 1
    )
    new_cache = lax.all_to_all(
        jnp.take(mine_part, sources, axis=0), "seq", split_axis=0, concat_axis=0, tiled=True
    )
    return (mixed, new_cache)


def solution(mesh):
    in_specs = (
        P("seq", "tp"),
        P(),
        P(None, "tp"),
        P(),
        P("tp", None),
        P("seq"),
        P("seq"),
        P("seq", None),
        P("seq", None),
        P("seq", "tp", None),
    )
    out_specs = (P("seq", "tp"), P("seq", "tp", None))
    return jax.shard_map(body, mesh=mesh, in_specs=in_specs, out_specs=out_specs, check_vma=False)
```

profile of v0, /device:TPU:1, one launch (start us, length us, event | category | flops | bytes accessed | tf_op | source)
XLA Modules:
  0.0 154.8 jit_solution(5848110831717273681)
XLA Ops:
  7.2 0.7 all-gather.3.cloned.1.call-update
  8.0 0.7 all-gather.5.cloned.1.call-update
  9.3 0.7 compare_and_fusion.1
  10.0 0.1 broadcast_in_dim.70
  10.1 0.1 broadcast_in_dim.71
  10.8 0.7 fusion.15
  11.5 1.8 %iota_compare_fusion = pred[512,2048]{0,1:T(8,128)(4,1)} fusion(s32[512]{0:T(512)S(1)} %iota_add_fusion), kind=kLoop, calls=%fused_computation.18 | loop fusion | flops 1048576 | bytes 1050624 | tf_op jit(solution)/shard_map/le | solution.py:66
  13.3 27.9 %all-gather.3.cloned.1.call-done = bf16[64,32,256]{2,1,0:T(8,128)(2,1)} async-done(((bf16[64,8,256]{2,1,0:T(8,128)(2,1)}), bf16[64,32,256]{2,1,0:T(8,128)(2,1)}) %all-gather.3.cloned.1.call-update) | async-done | bytes 1048592 | tf_op jit(solution)/shard_map/all_gather | solution.py:37
  41.2 11.5 %all-to-all-start = ((bf16[64,32,256]{2,1,0:T(8,128)(2,1)}), bf16[64,32,256]{2,1,0:T(8,128)(2,1)S(1)}, u32[]{:S(2)}, u32[]{:S(2)}) async-start(bf16[64,32,256]{2,1,0:T(8,128)(2,1)} %all-gather.3.cloned.1.call-done), calls=%async_computation | async-start | bytes 2097152 | tf_op jit(solution)/shard_map/all_to_all | solution.py:38
  52.8 25.5 %all-gather.5.cloned.1.call-done = bf16[512,2048]{1,0:T(8,128)(2,1)} async-done(((bf16[512,512]{1,0:T(8,128)(2,1)}), bf16[512,2048]{1,0:T(8,128)(2,1)}) %all-gather.5.cloned.1.call-update) | async-done | bytes 2097168 | tf_op jit(solution)/shard_map/all_gather | solution.py:30
  78.3 2.1 %convert_reduce_fusion = f32[512]{0:T(512)S(1)} fusion(bf16[512,2048]{1,0:T(8,128)(2,1)} %all-gather.5.cloned.1.call-done), kind=kLoop, calls=%fused_computation.12 | loop fusion | flops 2096640 | bytes 2099200 | tf_op jit(solution)/shard_map/reduce_sum | solution.py:12
  80.4 2.3 %fusion.8 = f32[512]{0:T(512)S(1)} fusion(bf16[512,2048]{1,0:T(8,128)(2,1)} %all-gather.5.cloned.1.call-done, f32[512]{0:T(512)S(1)} %broadcast_multiply_fusion), kind=kLoop, calls=%fused_computation.15 | loop fusion | flops 4193792 | bytes 2101248 | tf_op jit(solution)/shard_map/reduce_sum | solution.py:14
  82.8 0.7 fusion.10
  83.5 0.7 convolution_convert_fusion.2
  84.2 0.1 copy-done.5
  84.3 2.1 %convolution_convert_fusion.1 = bf16[512,512]{0,1:T(8,128)(2,1)} fusion(bf16[512,2048]{1,0:T(8,128)(2,1)S(1)} %fusion.10, bf16[2048,512]{1,0:T(8,128)(2,1)S(1)} %copy-done.5), kind=kOutput, calls=%fused_computation.21 | convolution fusion | flops 1074003968 | bytes 4718592 | tf_op jit(solution)/shard_map/dot_general | solution.py:32
  86.4 1.6 %gather_fusion = bf16[64,32,256]{2,1,0:T(8,128)(2,1)} fusion(bf16[64,32,256]{2,1,0:T(8,128)(2,1)S(1)} %all-to-all-done, s32[1024]{0:T(1024)S(1)} %pad_clamp_fusion.1), kind=kCustom, calls=%fused_computation | custom fusion | bytes 2097408 | tf_op jit(solution)/shard_map/jit(_take)/gather | solution.py:39
  88.0 1.5 bitcast_select_fusion.4
  89.5 1.9 %dynamic_update_slice.3 = bf16[2048,256]{1,0:T(8,128)(2,1)S(1)} dynamic-update-slice(bf16[2048,256]{1,0:T(8,128)(2,1)S(1)} %bitcast_select_fusion.4, bf16[512,256]{1,0:T(8,128)(2,1)S(1)} %convolution_convert_fusion.2, s32[]{:T(128)S(6)} %select_n.65, s32[]{:T(128)} %constant.15.clone.1) | dynamic-update-slice | bytes 524292 | tf_op jit(solution)/shard_map/dynamic_update_slice | solution.py:54
  91.4 1.2 broadcast_select_fusion
  92.6 10.7 %fusion.19 = (f32[4,512]{1,0:T(4,128)S(1)}, f32[4,512,2048]{1,2,0:T(8,128)}) fusion(pred[512,2048]{0,1:T(8,128)(4,1)} %iota_compare_fusion, bf16[512,4,128]{0,2,1:T(8,128)(2,1)} %bitcast.63, bf16[2048,256]{1,0:T(8,128)(2,1)} %broadcast_select_fusion), kind=kOutput, calls=%fused_computation.51 | convolution fusion | flops 1090521088 | bytes 18882560 | tf_op jit(solution)/shard_map/sub | solution.py:69
  103.4 7.0 %fusion.13 = bf16[128,4,512]{2,0,1:T(8,128)(2,1)S(1)} fusion(f32[4,512,2048]{1,2,0:T(8,128)} %get-tuple-element.3, f32[4,512]{1,0:T(4,128)S(1)} %get-tuple-element.2, bf16[2048,256]{1,0:T(8,128)(2,1)S(1)} %copy-done.3), kind=kOutput, calls=%fused_computation.22 | convolution fusion | flops 1082392576 | bytes 17833984 | tf_op jit(solution)/shard_map/htk,kd->thd/dot_general | solution.py:71
  110.4 2.6 %convolution_convert_fusion = bf16[512,2048]{1,0:T(8,128)(2,1)} fusion(bf16[512,512]{0,1:T(8,128)(2,1)S(1)} %bitcast.64, bf16[512,2048]{1,0:T(8,128)(2,1)S(1)} %copy-done), kind=kOutput, calls=%fused_computation.19 | convolution fusion | flops 1074790400 | bytes 4718592 | tf_op jit(solution)/shard_map/dot_general | solution.py:75
  113.1 0.1 select_reduce_fusion
  113.2 1.0 constant_dynamic-slice_fusion
  114.2 0.6 gather_fusion.1
  114.8 0.8 broadcast_select_fusion.1
  115.7 10.6 %all-to-all-start.1 = ((bf16[64,8,256]{2,1,0:T(8,128)(2,1)}), bf16[64,8,256]{2,1,0:T(8,128)(2,1)S(1)}, u32[]{:S(2)}, u32[]{:S(2)}) async-start(bf16[64,8,256]{2,1,0:T(8,128)(2,1)} %broadcast_select_fusion.1), calls=%async_computation.2 | async-start | bytes 524288 | tf_op jit(solution)/shard_map/all_to_all | solution.py:84
  126.3 13.1 %all-to-all-done.1 = bf16[64,8,256]{2,1,0:T(8,128)(2,1)S(1)} async-done(((bf16[64,8,256]{2,1,0:T(8,128)(2,1)}), bf16[64,8,256]{2,1,0:T(8,128)(2,1)S(1)}, u32[]{:S(2)}, u32[]{:S(2)}) %all-to-all-start.1) | async-done | bytes 262176 | tf_op jit(solution)/shard_map/all_to_all | solution.py:84
  139.5 6.1 %reduce-scatter.2.cloned.1.call-done = bf16[512,512]{1,0:T(8,128)(2,1)} async-done(((bf16[512,2048]{1,0:T(8,128)(2,1)}), bf16[512,512]{1,0:T(8,128)(2,1)}) %reduce-scatter.2.cloned.1.call-update) | async-done | bytes 524304 | tf_op jit(solution)/shard_map/reduce_scatter | solution.py:76
  145.6 2.0 %select_convert_fusion = bf16[512,512]{1,0:T(8,128)(2,1)} fusion(bf16[512,512]{1,0:T(8,128)(2,1)} %reduce-scatter.2.cloned.1.call-done, bf16[512,512]{1,0:T(8,128)(2,1)S(1)} %copy-done.2, pred[512]{0:T(512)(128)(4,1)S(1)} %iota_compare_fusion.3), kind=kLoop, calls=%fused_computation.25 | loop fusion | flops 1310720 | bytes 1573376 | tf_op jit(solution)/shard_map/convert_element_type | solution.py:80
  147.6 0.7 copy.29
  (29 shorter events, 0.2 us)
Async XLA Ops:
  7.2 103.3 %copy-start = (bf16[512,2048]{1,0:T(8,128)(2,1)S(1)}, bf16[512,2048]{1,0:T(8,128)(2,1)}, u32[]{:S(2)}) copy-start(bf16[512,2048]{1,0:T(8,128)(2,1)} %param.14) | copy-start | bytes 6291460
  7.2 75.6 %copy-start.4 = (f32[2048]{0:T(1024)S(1)}, f32[2048]{0:T(1024)}, u32[]{:S(2)}) copy-start(f32[2048]{0:T(1024)} %param.11) | copy-start | bytes 24580
  7.2 34.0 %all-gather.3.cloned.1.call-start = ((), (), s32[]{:S(2)}) async-start(), calls=%async_computation.3 | async-start | bytes 1310720 | tf_op jit(solution)/shard_map/all_gather | solution.py:37
  7.9 70.4 %all-gather.5.cloned.1.call-start = ((), (), s32[]{:S(2)}) async-start(), calls=%async_computation.4 | async-start | bytes 2621440 | tf_op jit(solution)/shard_map/all_gather | solution.py:30
  41.2 45.2 %all-to-all-start = ((bf16[64,32,256]{2,1,0:T(8,128)(2,1)}), bf16[64,32,256]{2,1,0:T(8,128)(2,1)S(1)}, u32[]{:S(2)}, u32[]{:S(2)}) async-start(bf16[64,32,256]{2,1,0:T(8,128)(2,1)} %all-gather.3.cloned.1.call-done), calls=%async_computation | async-start | bytes 2097152 | tf_op jit(solution)/shard_map/all_to_all | solution.py:38
  52.8 92.8 %reduce-scatter.2.cloned.1.call-start = ((), (), s32[]{:S(2)}) async-start(), calls=%async_computation.5 | async-start | bytes 2621440 | tf_op jit(solution)/shard_map/reduce_scatter | solution.py:76
  78.3 4.4 %copy-start.1 = (bf16[512,2048]{1,0:T(8,128)(2,1)S(1)}, bf16[512,2048]{1,0:T(8,128)(2,1)}, u32[]{:S(2)}) copy-start(bf16[512,2048]{1,0:T(8,128)(2,1)} %all-gather.5.cloned.1.call-done) | copy-start | bytes 6291460
  78.3 5.1 %copy-start.6 = (bf16[2048,256]{1,0:T(8,128)(2,1)S(1)}, bf16[2048,256]{1,0:T(8,128)(2,1)}, u32[]{:S(2)}) copy-start(bf16[2048,256]{1,0:T(8,128)(2,1)} %param.13) | copy-start | bytes 3145732
  82.7 1.6 %copy-start.5 = (bf16[2048,512]{1,0:T(8,128)(2,1)S(1)}, bf16[2048,512]{1,0:T(8,128)(2,1)}, u32[]{:S(2)}) copy-start(bf16[2048,512]{1,0:T(8,128)(2,1)} %param.12) | copy-start | bytes 6291460
  92.6 10.7 %copy-start.3 = (bf16[2048,256]{1,0:T(8,128)(2,1)S(1)}, bf16[2048,256]{1,0:T(8,128)(2,1)}, u32[]{:S(2)}) copy-start(bf16[2048,256]{1,0:T(8,128)(2,1)} %broadcast_select_fusion) | copy-start | bytes 3145732
  110.4 2.7 %copy-start.7 = (s32[1,64]{1,0:T(1,128)S(1)}, s32[1,64]{1,0:T(1,128)}, u32[]{:S(2)}) copy-start(s32[1,64]{1,0:T(1,128)} %param.18) | copy-start | bytes 772
  110.4 35.1 %copy-start.2 = (bf16[512,512]{1,0:T(8,128)(2,1)S(1)}, bf16[512,512]{1,0:T(8,128)(2,1)}, u32[]{:S(2)}) copy-start(bf16[512,512]{1,0:T(8,128)(2,1)} %param.10) | copy-start | bytes 1572868
  115.7 23.8 %all-to-all-start.1 = ((bf16[64,8,256]{2,1,0:T(8,128)(2,1)}), bf16[64,8,256]{2,1,0:T(8,128)(2,1)S(1)}, u32[]{:S(2)}, u32[]{:S(2)}) async-start(bf16[64,8,256]{2,1,0:T(8,128)(2,1)} %broadcast_select_fusion.1), calls=%async_computation.2 | async-start | bytes 524288 | tf_op jit(solution)/shard_map/all_to_all | solution.py:84
Sparse Core Ops, SparseCore 0:
  9.8 31.3 all-gather.2
  43.0 35.2 all-gather.4
  113.2 32.3 reduce-scatter.1
where the time goes:
time: 155 us
  waiting for transfers between devices  74.1 us (48%)
  matrix products  23.2 us (15%)
  starting transfers between devices  22.3 us (14%)
  between operations  15.3 us (10%)
  other arithmetic  13.9 us (9%)
  local copies, waits for them, and re-layouts  6.07 us (4%)
    all_gather x1, waiting for transfers between devices, body(): pooled = lax.all_gather(old_cache, 'tp', axis=1, tiled=True)  27.9 us
    all_gather x1, waiting for transfers between devices, body(): full_rows = lax.all_gather(tokens, 'tp', axis=1, tiled=True)  25.5 us
    all_to_all x1, waiting for transfers between devices, body(): lax.all_to_all(jnp.take(mine_part, sources, axis=0), 'seq', split_axis=0,...  13.1 us
    all_to_all x1, starting transfers between devices, body(): lax.all_to_all(pooled, 'seq', split_axis=0, concat_axis=0, tiled=True)  11.5 us
    sub x1, matrix products, body(): weights = jnp.exp(scores - top)  10.7 us
    all_to_all x1, starting transfers between devices, body(): lax.all_to_all(jnp.take(mine_part, sources, axis=0), 'seq', split_axis=0,...  10.6 us
    dot_general x1, matrix products, body(): jnp.einsum('htk,kd->thd', probs, values, preferred_element_type=jnp.float32)  7.05 us
    reduce_scatter x1, waiting for transfers between devices, body(): lax.psum_scatter(partial_out.astype(jnp.bfloat16), 'tp', scatter_dimensio...  6.08 us
  transfers between devices with their start and end apart: 5, of which 4 were waited for; matrix products, arithmetic and copies ran while one was open for 9% of the time, Pallas kernels for 0%

commit v1 on v0

--- a/solution.py
+++ b/solution.py
@@ -1,3 +1,4 @@
+import functools
 import jax
 import jax.numpy as jnp
 from jax import lax
@@ -5,6 +6,37 @@
 
 EPSILON = 1e-05
 MASKED = -1e30
+
+
+def _extend_trees(point, lane_axis):
+    out_arr, parts_out, a_next = (lax.psum(1, lane_axis), lax.axis_index(lane_axis), point.shape[1])
+    r2 = lax.dynamic_update_slice_in_dim(
+        jnp.zeros(
+            [d * out_arr if dev_j == 1 else d for dev_j, d in enumerate(point.shape)], point.dtype
+        ),
+        point,
+        parts_out * a_next,
+        axis=1,
+    )
+    view_out = x_new = point
+    for u in range(1, out_arr // 2 + 1):
+        view_out = lax.ppermute(
+            view_out, lane_axis, [(dev_j, (dev_j + 1) % out_arr) for dev_j in range(out_arr)]
+        )
+        r2 = lax.dynamic_update_slice_in_dim(
+            r2, view_out, (parts_out - u) % out_arr * a_next, axis=1
+        )
+        if 2 * u < out_arr:
+            x_new = lax.ppermute(
+                x_new, lane_axis, [(dev_j, (dev_j - 1) % out_arr) for dev_j in range(out_arr)]
+            )
+            r2 = lax.dynamic_update_slice_in_dim(
+                r2, x_new, (parts_out + u) % out_arr * a_next, axis=1
+            )
+    return r2
+
+
+press_ticks_over_axis = functools.partial(_extend_trees, lane_axis="tp")
 
 
 def normalize(rows, norm_gain):
@@ -34,7 +66,7 @@
     groups = lax.axis_size("seq")
     tp_count = lax.axis_size("tp")
     holders = old_table[0]
-    pooled = lax.all_gather(old_cache, "tp", axis=1, tiled=True)
+    pooled = press_ticks_over_axis(old_cache)
     arrived = lax.all_to_all(pooled, "seq", split_axis=0, concat_axis=0, tiled=True)
     ordered = jnp.take(arrived, holders, axis=0)
     block_rows = ordered.shape[1]

time: 155 us -> 139 us (0.90)
  waiting for transfers between devices: 74.1 us -> 46.9 us
  starting transfers between devices: 22.3 us -> 29.1 us
  local copies, waits for them, and re-layouts: 6.07 us -> 11.2 us
    all_gather x1 -> x0, waiting for transfers between devices: 27.9 us -> none  [body(): pooled = lax.all_gather(old_cache, 'tp', axis=1, tiled=True)]
    all_gather x1, waiting for transfers between devices: 25.5 us -> 0.02 us  [body(): full_rows = lax.all_gather(tokens, 'tp', axis=1, tiled=True)]
    all_to_all x1, waiting for transfers between devices: 0.01 us -> 24.3 us  [body(): lax.all_to_all(pooled, 'seq', split_axis=0, concat_axis=0, tiled=True)]
    ppermute x0 -> x3, starting transfers between devices: none -> 6.08 us  [the longest x2 3.98 us: _extend_trees(): lax.ppermute(view_out, lane_axis, [(dev_j, (dev_j + 1) % out_arr) for dev...]
    all_to_all x1, starting transfers between devices: 11.5 us -> 16.3 us  [body(): lax.all_to_all(pooled, 'seq', split_axis=0, concat_axis=0, tiled=True)]
    ppermute x0 -> x3, waiting for transfers between devices: none -> 4.31 us  [the longest x2 4.31 us: _extend_trees(): lax.ppermute(view_out, lane_axis, [(dev_j, (dev_j + 1) % out_arr) for dev...]
    all_to_all x1, starting transfers between devices: 10.6 us -> 6.45 us  [body(): lax.all_to_all(jnp.take(mine_part, sources, axis=0), 'seq', split_axis=0,...]
    dynamic_update_slice x0 -> x4, local copies, waits for them, and re-layouts: none -> 3.99 us  [the longest x1 1.7 us: _extend_trees(): lax.dynamic_update_slice_in_dim(jnp.zeros([d * out_arr if dev_j == 1 else...]
  transfers between devices with their start and end apart: 5 -> 7, of which waited for: 4 -> 5; matrix products, arithmetic and copies ran while one was open for 9% -> 9% of each run, Pallas kernels for 0% -> 0%
where the time goes in v1:
time: 139 us
  waiting for transfers between devices  46.9 us (34%)
  starting transfers between devices  29.1 us (21%)
  matrix products  23.2 us (17%)
  between operations  15.6 us (11%)
  other arithmetic  12.6 us (9%)
  local copies, waits for them, and re-layouts  11.2 us (8%)
    all_to_all x1, waiting for transfers between devices, body(): lax.all_to_all(pooled, 'seq', split_axis=0, concat_axis=0, tiled=True)  24.3 us
    all_to_all x1, starting transfers between devices, body(): lax.all_to_all(pooled, 'seq', split_axis=0, concat_axis=0, tiled=True)  16.3 us
    all_to_all x1, waiting for transfers between devices, body(): lax.all_to_all(jnp.take(mine_part, sources, axis=0), 'seq', split_axis=0,...  13.1 us
    sub x1, matrix products, body(): weights = jnp.exp(scores - top)  10.7 us
    dot_general x1, matrix products, body(): jnp.einsum('htk,kd->thd', probs, values, preferred_element_type=jnp.float32)  7.05 us
    all_to_all x1, starting transfers between devices, body(): lax.all_to_all(jnp.take(mine_part, sources, axis=0), 'seq', split_axis=0,...  6.45 us
    reduce_scatter x1, waiting for transfers between devices, body(): lax.psum_scatter(partial_out.astype(jnp.bfloat16), 'tp', scatter_dimensio...  5.11 us
    ppermute x2, waiting for transfers between devices, _extend_trees(): lax.ppermute(view_out, lane_axis, [(dev_j, (dev_j + 1) % out_arr) for dev...  4.31 us
  transfers between devices with their start and end apart: 7, of which 5 were waited for; matrix products, arithmetic and copies ran while one was open for 9% of the time, Pallas kernels for 0%

profile of v1, /device:TPU:1, one launch (start us, length us, event | category | flops | bytes accessed | tf_op | source)
XLA Modules:
  0.0 138.6 jit_solution(15472733806858056502)
XLA Ops:
  7.2 2.2 %collective-permute-start = (bf16[64,8,256]{2,1,0:T(8,128)(2,1)}, bf16[64,8,256]{2,1,0:T(8,128)(2,1)S(1)}, u32[]{:S(2)}, u32[]{:S(2)}) collective-permute-start(bf16[64,8,256]{2,1,0:T(8,128)(2,1)} %param.19), channel_id=1, source_target_pairs={{0,1},{1,2},{2,3},{3,0},{4,5},{5,6},{6,7},{7,4},{8,9},{9,10},{10,1... | collective-permute-start | bytes 786440 | tf_op jit(solution)/shard_map/ppermute | solution.py:23
  9.5 2.1 %collective-permute-start.1 = (bf16[64,8,256]{2,1,0:T(8,128)(2,1)}, bf16[64,8,256]{2,1,0:T(8,128)(2,1)S(1)}, u32[]{:S(2)}, u32[]{:S(2)}) collective-permute-start(bf16[64,8,256]{2,1,0:T(8,128)(2,1)} %param.19), channel_id=1, source_target_pairs={{0,3},{1,0},{2,1},{3,2},{4,7},{5,4},{6,5},{7,6},{8,11},{9,8},{10,9... | collective-permute-start | bytes 786440 | tf_op jit(solution)/shard_map/ppermute | solution.py:30
  11.6 3.3 %collective-permute-done = bf16[64,8,256]{2,1,0:T(8,128)(2,1)S(1)} collective-permute-done((bf16[64,8,256]{2,1,0:T(8,128)(2,1)}, bf16[64,8,256]{2,1,0:T(8,128)(2,1)S(1)}, u32[]{:S(2)}, u32[]{:S(2)}) %collective-permute-start) | collective-permute-done | bytes 262176 | tf_op jit(solution)/shard_map/ppermute | solution.py:23
  14.9 1.8 %collective-permute-start.2 = (bf16[64,8,256]{2,1,0:T(8,128)(2,1)S(1)}, bf16[64,8,256]{2,1,0:T(8,128)(2,1)S(1)}, u32[]{:S(2)}, u32[]{:S(2)}) collective-permute-start(bf16[64,8,256]{2,1,0:T(8,128)(2,1)S(1)} %collective-permute-done), channel_id=1, source_target_pairs={{0,1},{1,2},{2,3},{3,0},{4,5},{5,6},{6,7},{7,4},{8,9},{9,10},{10,1... | collective-permute-start | bytes 786440 | tf_op jit(solution)/shard_map/ppermute | solution.py:23
  16.6 1.1 broadcast_in_dim.76
  17.8 1.7 %constant_dynamic-update-slice_fusion.3 = bf16[64,32,256]{2,1,0:T(8,128)(2,1)} fusion(bf16[64,32,256]{2,1,0:T(8,128)(2,1)} %broadcast_in_dim.76, bf16[64,8,256]{2,1,0:T(8,128)(2,1)} %param.19, s32[]{:T(128)S(6)} %select_n.88), kind=kLoop, calls=%fused_computation.49 | loop fusion | bytes 524292 | tf_op jit(solution)/shard_map/dynamic_update_slice | solution.py:13
  19.5 0.8 constant_dynamic-update-slice_fusion.2
  20.3 0.7 constant_dynamic-update-slice_fusion.1
  21.0 1.0 collective-permute-done.2
  22.0 0.8 constant_dynamic-update-slice_fusion
  22.8 16.3 %all-to-all-start = ((bf16[64,32,256]{2,1,0:T(8,128)(2,1)}), bf16[64,32,256]{2,1,0:T(8,128)(2,1)S(1)}, u32[]{:S(2)}, u32[]{:S(2)}) async-start(bf16[64,32,256]{2,1,0:T(8,128)(2,1)} %constant_dynamic-update-slice_fusion), calls=%async_computation | async-start | bytes 2097152 | tf_op jit(solution)/shard_map/all_to_all | solution.py:70
  41.0 1.8 %iota_compare_fusion = pred[512,2048]{0,1:T(8,128)(4,1)} fusion(s32[512]{0:T(512)S(1)} %iota_add_fusion), kind=kLoop, calls=%fused_computation.18 | loop fusion | flops 1048576 | bytes 1050624 | tf_op jit(solution)/shard_map/le | solution.py:98
  42.8 24.3 %all-to-all-done = bf16[64,32,256]{2,1,0:T(8,128)(2,1)S(1)} async-done(((bf16[64,32,256]{2,1,0:T(8,128)(2,1)}), bf16[64,32,256]{2,1,0:T(8,128)(2,1)S(1)}, u32[]{:S(2)}, u32[]{:S(2)}) %all-to-all-start) | async-done | bytes 1048608 | tf_op jit(solution)/shard_map/all_to_all | solution.py:70
  67.1 1.6 %gather_fusion = bf16[64,32,256]{2,1,0:T(8,128)(2,1)} fusion(bf16[64,32,256]{2,1,0:T(8,128)(2,1)S(1)} %all-to-all-done, s32[1024]{0:T(1024)S(1)} %pad_clamp_fusion.1), kind=kCustom, calls=%fused_computation | custom fusion | bytes 2097408 | tf_op jit(solution)/shard_map/jit(_take)/gather | solution.py:71
  68.7 1.5 %bitcast_select_fusion.4 = bf16[2048,256]{1,0:T(8,128)(2,1)S(1)} fusion(bf16[64,32,256]{2,1,0:T(8,128)(2,1)} %gather_fusion, pred[2048]{0:T(1024)(128)(4,1)S(1)} %broadcast_in_dim.74), kind=kLoop, calls=%fused_computation.24 | loop fusion | flops 524288 | bytes 2099200 | tf_op jit(solution)/shard_map/jit(_take)/select_n | solution.py:71
  70.2 2.1 %convert_reduce_fusion = f32[512]{0:T(512)S(1)} fusion(bf16[512,2048]{1,0:T(8,128)(2,1)} %all-gather.2.cloned.1.call-done), kind=kLoop, calls=%fused_computation.12 | loop fusion | flops 2096640 | bytes 2099200 | tf_op jit(solution)/shard_map/reduce_sum | solution.py:44
  72.3 2.3 %fusion.8 = f32[512]{0:T(512)S(1)} fusion(bf16[512,2048]{1,0:T(8,128)(2,1)} %all-gather.2.cloned.1.call-done, f32[512]{0:T(512)S(1)} %broadcast_multiply_fusion), kind=kLoop, calls=%fused_computation.15 | loop fusion | flops 4193792 | bytes 2101248 | tf_op jit(solution)/shard_map/reduce_sum | solution.py:46
  74.6 0.7 fusion.10
  75.3 0.7 convolution_convert_fusion.2
  76.2 2.1 %convolution_convert_fusion.1 = bf16[512,512]{0,1:T(8,128)(2,1)} fusion(bf16[512,2048]{1,0:T(8,128)(2,1)S(1)} %fusion.10, bf16[2048,512]{1,0:T(8,128)(2,1)S(1)} %copy-done.6), kind=kOutput, calls=%fused_computation.21 | convolution fusion | flops 1074003968 | bytes 4718592 | tf_op jit(solution)/shard_map/dot_general | solution.py:64
  78.3 1.8 %dynamic_update_slice.19 = bf16[2048,256]{1,0:T(8,128)(2,1)S(1)} dynamic-update-slice(bf16[2048,256]{1,0:T(8,128)(2,1)S(1)} %bitcast_select_fusion.4, bf16[512,256]{1,0:T(8,128)(2,1)S(1)} %convolution_convert_fusion.2, s32[]{:T(128)S(6)} %select_n.97, s32[]{:T(128)} %constant.64.clone.1) | dynamic-update-slice | bytes 524292 | tf_op jit(solution)/shard_map/dynamic_update_slice | solution.py:86
  80.1 1.3 broadcast_select_fusion
  81.4 10.7 %fusion.19 = (f32[4,512]{1,0:T(4,128)S(1)}, f32[4,512,2048]{1,2,0:T(8,128)}) fusion(pred[512,2048]{0,1:T(8,128)(4,1)} %iota_compare_fusion, bf16[512,4,128]{0,2,1:T(8,128)(2,1)} %bitcast.63, bf16[2048,256]{1,0:T(8,128)(2,1)} %broadcast_select_fusion), kind=kOutput, calls=%fused_computation.55 | convolution fusion | flops 1090521088 | bytes 18882560 | tf_op jit(solution)/shard_map/sub | solution.py:101
  92.1 7.0 %fusion.13 = bf16[128,4,512]{2,0,1:T(8,128)(2,1)S(1)} fusion(f32[4,512,2048]{1,2,0:T(8,128)} %get-tuple-element.3, f32[4,512]{1,0:T(4,128)S(1)} %get-tuple-element.2, bf16[2048,256]{1,0:T(8,128)(2,1)S(1)} %copy-done.3), kind=kOutput, calls=%fused_computation.22 | convolution fusion | flops 1082392576 | bytes 17833984 | tf_op jit(solution)/shard_map/htk,kd->thd/dot_general | solution.py:103
  99.2 2.6 %convolution_convert_fusion = bf16[512,2048]{1,0:T(8,128)(2,1)} fusion(bf16[512,512]{0,1:T(8,128)(2,1)S(1)} %bitcast.64, bf16[512,2048]{1,0:T(8,128)(2,1)S(1)} %copy-done), kind=kOutput, calls=%fused_computation.19 | convolution fusion | flops 1074790400 | bytes 4718592 | tf_op jit(solution)/shard_map/dot_general | solution.py:107
  101.9 1.0 constant_dynamic-slice_fusion
  103.5 0.8 broadcast_select_fusion.1
  104.3 6.4 %all-to-all-start.1 = ((bf16[64,8,256]{2,1,0:T(8,128)(2,1)}), bf16[64,8,256]{2,1,0:T(8,128)(2,1)S(1)}, u32[]{:S(2)}, u32[]{:S(2)}) async-start(bf16[64,8,256]{2,1,0:T(8,128)(2,1)} %broadcast_select_fusion.1), calls=%async_computation.2 | async-start | bytes 524288 | tf_op jit(solution)/shard_map/all_to_all | solution.py:116
  110.8 13.1 %all-to-all-done.1 = bf16[64,8,256]{2,1,0:T(8,128)(2,1)S(1)} async-done(((bf16[64,8,256]{2,1,0:T(8,128)(2,1)}), bf16[64,8,256]{2,1,0:T(8,128)(2,1)S(1)}, u32[]{:S(2)}, u32[]{:S(2)}) %all-to-all-start.1) | async-done | bytes 262176 | tf_op jit(solution)/shard_map/all_to_all | solution.py:116
  123.9 5.1 %reduce-scatter.2.cloned.1.call-done = bf16[512,512]{1,0:T(8,128)(2,1)} async-done(((bf16[512,2048]{1,0:T(8,128)(2,1)}), bf16[512,512]{1,0:T(8,128)(2,1)}) %reduce-scatter.2.cloned.1.call-update) | async-done | bytes 524304 | tf_op jit(solution)/shard_map/reduce_scatter | solution.py:108
  129.0 2.0 %select_convert_fusion = bf16[512,512]{1,0:T(8,128)(2,1)} fusion(bf16[512,512]{1,0:T(8,128)(2,1)} %reduce-scatter.2.cloned.1.call-done, bf16[512,512]{1,0:T(8,128)(2,1)S(1)} %copy-done.2, pred[512]{0:T(512)(128)(4,1)S(1)} %iota_compare_fusion.3), kind=kLoop, calls=%fused_computation.25 | loop fusion | flops 1310720 | bytes 1573376 | tf_op jit(solution)/shard_map/convert_element_type | solution.py:112
  131.0 0.7 copy.33
  (38 shorter events, 1.4 us)
Async XLA Ops:
  7.2 92.0 %copy-start = (bf16[512,2048]{1,0:T(8,128)(2,1)S(1)}, bf16[512,2048]{1,0:T(8,128)(2,1)}, u32[]{:S(2)}) copy-start(bf16[512,2048]{1,0:T(8,128)(2,1)} %param.14) | copy-start | bytes 6291460
  7.2 32.1 %copy-start.8 = (s32[1,64]{1,0:T(1,128)S(1)}, s32[1,64]{1,0:T(1,128)}, u32[]{:S(2)}) copy-start(s32[1,64]{1,0:T(1,128)} %param.18) | copy-start | bytes 772
  7.2 32.2 %copy-start.5 = (s32[1,64]{1,0:T(1,128)S(1)}, s32[1,64]{1,0:T(1,128)}, u32[]{:S(2)}) copy-start(s32[1,64]{1,0:T(1,128)} %param.17) | copy-start | bytes 772
  7.2 63.0 %all-gather.2.cloned.1.call-start = ((), (), s32[]{:S(2)}) async-start(), calls=%async_computation.3 | async-start | bytes 2621440 | tf_op jit(solution)/shard_map/all_gather | solution.py:62
  7.2 7.6 %collective-permute-start = (bf16[64,8,256]{2,1,0:T(8,128)(2,1)}, bf16[64,8,256]{2,1,0:T(8,128)(2,1)S(1)}, u32[]{:S(2)}, u32[]{:S(2)}) collective-permute-start(bf16[64,8,256]{2,1,0:T(8,128)(2,1)} %param.19), channel_id=1, source_target_pairs={{0,1},{1,2},{2,3},{3,0},{4,5},{5,6},{6,7},{7,4},{8,9},{9,10},{10,1... | collective-permute-start | bytes 786440 | tf_op jit(solution)/shard_map/ppermute | solution.py:23
  9.5 10.8 %collective-permute-start.1 = (bf16[64,8,256]{2,1,0:T(8,128)(2,1)}, bf16[64,8,256]{2,1,0:T(8,128)(2,1)S(1)}, u32[]{:S(2)}, u32[]{:S(2)}) collective-permute-start(bf16[64,8,256]{2,1,0:T(8,128)(2,1)} %param.19), channel_id=1, source_target_pairs={{0,3},{1,0},{2,1},{3,2},{4,7},{5,4},{6,5},{7,6},{8,11},{9,8},{10,9... | collective-permute-start | bytes 786440 | tf_op jit(solution)/shard_map/ppermute | solution.py:30
  14.9 7.2 %collective-permute-start.2 = (bf16[64,8,256]{2,1,0:T(8,128)(2,1)S(1)}, bf16[64,8,256]{2,1,0:T(8,128)(2,1)S(1)}, u32[]{:S(2)}, u32[]{:S(2)}) collective-permute-start(bf16[64,8,256]{2,1,0:T(8,128)(2,1)S(1)} %collective-permute-done), channel_id=1, source_target_pairs={{0,1},{1,2},{2,3},{3,0},{4,5},{5,6},{6,7},{7,4},{8,9},{9,10},{10,1... | collective-permute-start | bytes 786440 | tf_op jit(solution)/shard_map/ppermute | solution.py:23
  22.8 44.3 %all-to-all-start = ((bf16[64,32,256]{2,1,0:T(8,128)(2,1)}), bf16[64,32,256]{2,1,0:T(8,128)(2,1)S(1)}, u32[]{:S(2)}, u32[]{:S(2)}) async-start(bf16[64,32,256]{2,1,0:T(8,128)(2,1)} %constant_dynamic-update-slice_fusion), calls=%async_computation | async-start | bytes 2097152 | tf_op jit(solution)/shard_map/all_to_all | solution.py:70
  39.1 90.0 %reduce-scatter.2.cloned.1.call-start = ((), (), s32[]{:S(2)}) async-start(), calls=%async_computation.4 | async-start | bytes 2621440 | tf_op jit(solution)/shard_map/reduce_scatter | solution.py:108
  42.8 31.8 %copy-start.4 = (f32[2048]{0:T(1024)S(1)}, f32[2048]{0:T(1024)}, u32[]{:S(2)}) copy-start(f32[2048]{0:T(1024)} %param.11) | copy-start | bytes 24580
  70.2 4.4 %copy-start.1 = (bf16[512,2048]{1,0:T(8,128)(2,1)S(1)}, bf16[512,2048]{1,0:T(8,128)(2,1)}, u32[]{:S(2)}) copy-start(bf16[512,2048]{1,0:T(8,128)(2,1)} %all-gather.2.cloned.1.call-done) | copy-start | bytes 6291460
  70.2 5.1 %copy-start.7 = (bf16[2048,256]{1,0:T(8,128)(2,1)S(1)}, bf16[2048,256]{1,0:T(8,128)(2,1)}, u32[]{:S(2)}) copy-start(bf16[2048,256]{1,0:T(8,128)(2,1)} %param.13) | copy-start | bytes 3145732
  74.6 1.6 %copy-start.6 = (bf16[2048,512]{1,0:T(8,128)(2,1)S(1)}, bf16[2048,512]{1,0:T(8,128)(2,1)}, u32[]{:S(2)}) copy-start(bf16[2048,512]{1,0:T(8,128)(2,1)} %param.12) | copy-start | bytes 6291460
  81.4 10.7 %copy-start.3 = (bf16[2048,256]{1,0:T(8,128)(2,1)S(1)}, bf16[2048,256]{1,0:T(8,128)(2,1)}, u32[]{:S(2)}) copy-start(bf16[2048,256]{1,0:T(8,128)(2,1)} %broadcast_select_fusion) | copy-start | bytes 3145732
  99.2 29.9 %copy-start.2 = (bf16[512,512]{1,0:T(8,128)(2,1)S(1)}, bf16[512,512]{1,0:T(8,128)(2,1)}, u32[]{:S(2)}) copy-start(bf16[512,512]{1,0:T(8,128)(2,1)} %param.10) | copy-start | bytes 1572868
  104.3 19.6 %all-to-all-start.1 = ((bf16[64,8,256]{2,1,0:T(8,128)(2,1)}), bf16[64,8,256]{2,1,0:T(8,128)(2,1)S(1)}, u32[]{:S(2)}, u32[]{:S(2)}) async-start(bf16[64,8,256]{2,1,0:T(8,128)(2,1)} %broadcast_select_fusion.1), calls=%async_computation.2 | async-start | bytes 524288 | tf_op jit(solution)/shard_map/all_to_all | solution.py:116
Sparse Core Ops, SparseCore 0:
  9.8 37.2 all-gather.1
  102.0 27.0 reduce-scatter.1
